TPU v7x, 32 devices: a whole 2x2x4 slice. The times are simulated.
32 devices in a mesh: dp: 8 (over y, x, core), filter: 4 (over z).
Axes of the slice: x: 2, y: 2, z: 4, core: 2. Of those that a mesh axis runs over, the one named last changes fastest.
Arguments:
- inputs: bfloat16 [8, 48, 24, 1024], P('dp', None, None, 'filter'), may hold values from -6 to 6
- kernel: bfloat16 [3, 3, 1024, 1024], P(None, None, 'filter'), may hold values from -0.0625 to 0.0625
- cotangent: bfloat16 [8, 48, 24, 1024], P('dp', 'filter'), may hold values from -6 to 6
Outputs:
- outputs: bfloat16 [8, 48, 24, 1024], P('dp', 'filter')
- input_grad: bfloat16 [8, 48, 24, 1024], P('dp', None, None, 'filter')
- kernel_grad: float32 [1024, 3, 3, 1024], P('dp', None, None, 'filter')
All inputs are finite; a program needn't handle non-finite values.
Results may differ from a plain program's by a relative error of at most 0.001.
Values may be sent and summed in bfloat16 or wider, within the bound.
A program may use at most 128 MiB of HBM per device.

v0:
```python
import jax
import jax.numpy as jnp
from jax import lax
from jax.sharding import PartitionSpec as P


def conv_rows(xpad, weights, count, width):
    total = jnp.zeros((count, width, weights.shape[3]), jnp.float32)
    for a in range(3):
        for b in range(3):
            total = total + jnp.einsum(
                "hwi,io->hwo",
                xpad[a : a + count, b : b + width],
                weights[a, b],
                preferred_element_type=jnp.float32,
            )
    return total


def on_device(inputs, kernel, cotangent):
    sample = inputs[0]
    height = sample.shape[0]
    width = sample.shape[1]
    local_in = sample.shape[2]
    channels = kernel.shape[3]
    groups = lax.axis_size("filter")
    my_rows = height // groups
    xpad = jnp.pad(sample, ((1, 1), (1, 1), (0, 0)))
    summed = lax.psum_scatter(
        conv_rows(xpad, kernel, my_rows * lax.axis_size("filter"), width),
        "filter",
        scatter_dimension=0,
        tiled=True,
    )
    outputs = summed.astype(jnp.bfloat16)[None]
    start = jnp.int32(0)
    back_pad = jnp.zeros((height + 2, width + 2, local_in), jnp.float32)
    grad_rows = lax.all_gather(cotangent, "filter", axis=1, tiled=True)[0]
    count = grad_rows.shape[0]
    taps = []
    for a in range(3):
        for b in range(3):
            contrib = jnp.einsum(
                "hwo,io->hwi", grad_rows, kernel[a, b], preferred_element_type=jnp.float32
            )
            region = lax.dynamic_slice(back_pad, (start + a, b, 0), (count, width, local_in))
            back_pad = lax.dynamic_update_slice(back_pad, region + contrib, (start + a, b, 0))
            taps.append(
                jnp.einsum(
                    "hwi,hwo->oi",
                    xpad[a : a + count, b : b + width],
                    grad_rows,
                    preferred_element_type=jnp.float32,
                )
            )
    grads = jnp.stack(taps, 1).reshape(channels, 3, 3, local_in)
    back_pad, grads = (back_pad, grads)
    input_grad = back_pad[1:-1, 1:-1].astype(jnp.bfloat16)[None]
    samples = lax.axis_size("dp")
    scale = 1.0 / jnp.sqrt(jnp.float32(samples * height * width))
    mine = lax.psum_scatter(grads, "dp", scatter_dimension=0, tiled=True)
    return (outputs, input_grad, mine * scale)


def solution(mesh):
    return jax.shard_map(
        on_device,
        mesh=mesh,
        in_specs=(
            P("dp", None, None, "filter"),
            P(None, None, "filter", None),
            P("dp", "filter", None, None),
        ),
        out_specs=(
            P("dp", "filter", None, None),
            P("dp", None, None, "filter"),
            P("dp", None, None, "filter"),
        ),
        check_vma=False,
    )
```

profile of v0, /device:TPU:0, one launch (start us, length us, event | category | flops | bytes accessed | tf_op | source)
XLA Modules:
  0.0 238.2 jit_solution(5263941101948910231)
XLA Ops:
  7.2 0.0 all-gather.2.cloned.1.call-start
  7.2 0.7 all-gather.2.cloned.1.call-update
  7.9 0.0 reduce-scatter.3.cloned.1.call-start
  7.9 0.0 copy-start.1
  8.0 0.0 copy-start.3
  8.0 2.1 fusion.124
  10.1 0.0 copy-done.1
  10.1 0.7 copy-done.3
  10.8 0.8 fusion.127
  11.6 3.0 %fusion.130 = f32[48,24,1024]{2,1,0:T(8,128)} fusion(bf16[3,3,256,1024]{3,2,1,0:T(8,128)(2,1)S(1)} %copy-done.3, bf16[48,24,256]{2,1,0:T(8,128)(2,1)S(1)} %bitcast.238), kind=kOutput, calls=%fused_computation.86 | convolution fusion | flops 603979776 | bytes 5832704 | tf_op jit(solution)/shard_map/hwi,io->hwo/dot_general | solution.py:11
  14.6 3.0 %fusion.136 = f32[48,24,1024]{2,1,0:T(8,128)} fusion(bf16[3,3,256,1024]{3,2,1,0:T(8,128)(2,1)S(1)} %copy-done.3, bf16[48,24,256]{2,1,0:T(8,128)(2,1)S(1)} %bitcast.239), kind=kOutput, calls=%fused_computation.92 | convolution fusion | flops 603979776 | bytes 5832704 | tf_op jit(solution)/shard_map/hwi,io->hwo/dot_general | solution.py:11
  17.6 3.0 %fusion.139 = f32[48,24,1024]{2,1,0:T(8,128)} fusion(bf16[3,3,256,1024]{3,2,1,0:T(8,128)(2,1)S(1)} %copy-done.3, bf16[48,24,256]{2,1,0:T(8,128)(2,1)S(1)} %bitcast.240), kind=kOutput, calls=%fused_computation.95 | convolution fusion | flops 603979776 | bytes 5832704 | tf_op jit(solution)/shard_map/hwi,io->hwo/dot_general | solution.py:11
  20.6 2.9 %fusion.145 = f32[48,24,1024]{2,1,0:T(8,128)} fusion(bf16[3,3,256,1024]{3,2,1,0:T(8,128)(2,1)S(1)} %copy-done.3, bf16[48,24,256]{2,1,0:T(8,128)(2,1)S(1)} %bitcast.241), kind=kOutput, calls=%fused_computation.101 | convolution fusion | flops 603979776 | bytes 5832704 | tf_op jit(solution)/shard_map/hwi,io->hwo/dot_general | solution.py:11
  23.5 3.0 %fusion.142 = f32[48,24,1024]{2,1,0:T(8,128)} fusion(bf16[3,3,256,1024]{3,2,1,0:T(8,128)(2,1)S(1)} %copy-done.3, bf16[48,24,256]{2,1,0:T(8,128)(2,1)S(1)} %bitcast.242), kind=kOutput, calls=%fused_computation.98 | convolution fusion | flops 603979776 | bytes 5832704 | tf_op jit(solution)/shard_map/hwi,io->hwo/dot_general | solution.py:11
  26.5 2.9 %fusion.133 = f32[48,24,1024]{2,1,0:T(8,128)} fusion(bf16[3,3,256,1024]{3,2,1,0:T(8,128)(2,1)S(1)} %copy-done.3, bf16[1,48,24,256]{3,2,1,0:T(8,128)(2,1)S(1)} %copy-done.1), kind=kOutput, calls=%fused_computation.89 | convolution fusion | flops 603979776 | bytes 5832704 | tf_op jit(solution)/shard_map/hwi,io->hwo/dot_general | solution.py:11
  29.4 13.0 %add_add_fusion = f32[48,24,1024]{2,1,0:T(8,128)} fusion(f32[48,24,1024]{2,1,0:T(8,128)S(1)} %fusion.124, f32[48,24,1024]{2,1,0:T(8,128)S(1)} %fusion.127, f32[48,24,1024]{2,1,0:T(8,128)} %fusion.130, f32[48,24,1024]{2,1,0:T(8,128)} %fusion.133, f32[48,24,1024]{2,1,0:T(8,128)} %fusion.136, f32[48,24,1024]{2,1,0:T(8,128)} %fusion.139, ...), kind=kOutput, calls=%fused_computation | convolution fusion | flops 613416960 | bytes 43581440 | tf_op jit(solution)/shard_map/hwi,io->hwo/dot_general | solution.py:11
  42.4 0.0 reduce-scatter.3.cloned.1.call-update
  42.5 0.2 reduce-scatter.5.cloned.1.call-start
  42.7 19.6 %all-gather.2.cloned.1.call-done = bf16[1,48,24,1024]{3,2,0,1:T(8,128)(2,1)} async-done(((bf16[1,12,24,1024]{3,2,0,1:T(8,128)(2,1)}), bf16[1,48,24,1024]{3,2,0,1:T(8,128)(2,1)}) %all-gather.2.cloned.1.call-update) | async-done | bytes 2359312 | tf_op jit(solution)/shard_map/all_gather | solution.py:38
  62.3 0.0 copy-start
  62.3 2.7 %fusion.75 = f32[1024,9,256]{0,2,1:T(8,128)S(1)} fusion(bf16[1,48,24,1024]{3,2,0,1:T(8,128)(2,1)} %all-gather.2.cloned.1.call-done, bf16[48,24,256]{2,1,0:T(8,128)(2,1)S(1)} %bitcast.244), kind=kOutput, calls=%fused_computation.50 | convolution fusion | flops 603979776 | bytes 3997696 | tf_op jit(solution)/shard_map/hwi,hwo->oi/dot_general | solution.py:49
  65.0 0.0 copy-done
  65.0 0.9 fusion.81
  65.9 0.9 fusion.87
  66.7 0.9 fusion.93
  67.6 0.9 fusion.69
  68.5 0.9 fusion.99
  69.4 0.9 fusion.105
  70.3 0.9 fusion.111
  71.1 0.9 fusion.117
  72.0 0.0 copy-start.2
  72.0 3.6 %copy-done.2 = f32[1024,9,256]{0,2,1:T(8,128)} copy-done((f32[1024,9,256]{0,2,1:T(8,128)}, f32[1024,9,256]{0,2,1:T(8,128)S(1)}, u32[]{:S(2)}) %copy-start.2) | copy-done | bytes 9437208
  75.7 9.6 %copy.46 = f32[1024,3,3,256]{3,0,2,1:T(8,128)} copy(f32[1024,3,3,256]{0,3,2,1:T(8,128)} %bitcast.252) | data formatting | bytes 18874368 | tf_op jit(solution)/shard_map/reshape | solution.py:56
  85.3 0.0 reduce-scatter.5.cloned.1.call-update
  85.3 1.9 fusion.34
  87.2 1.4 dynamic_update_slice.27
  88.6 1.9 fusion.36
  90.5 7.0 %dynamic_update_slice.28 = f32[50,26,256]{2,1,0:T(8,128)} dynamic-update-slice(f32[50,26,256]{2,1,0:T(8,128)} %dynamic_update_slice.27, f32[48,24,256]{2,1,0:T(8,128)S(1)} %fusion.36, s32[]{:T(128)} %constant.3.clone.1, s32[]{:T(128)} %constant.4.clone.1, s32[]{:T(128)} %constant.3.clone.1) | dynamic-update-slice | bytes 2359300 | tf_op jit(solution)/shard_map/dynamic_update_slice | solution.py:47
  97.6 2.4 %fusion.39 = f32[48,24,256]{2,1,0:T(8,128)S(1)} fusion(bf16[1,48,24,1024]{3,2,0,1:T(8,128)(2,1)S(1)} %copy-done, f32[50,26,256]{2,1,0:T(8,128)} %dynamic_update_slice.28, bf16[3,3,256,1024]{3,2,1,0:T(8,128)(2,1)} %param.4), kind=kOutput, calls=%fused_computation.38 | convolution fusion | flops 604274688 | bytes 5242880 | tf_op jit(solution)/shard_map/hwo,io->hwi/dot_general | solution.py:43
  100.0 7.0 %dynamic_update_slice.29 = f32[50,26,256]{2,1,0:T(8,128)} dynamic-update-slice(f32[50,26,256]{2,1,0:T(8,128)} %dynamic_update_slice.28, f32[48,24,256]{2,1,0:T(8,128)S(1)} %fusion.39, s32[]{:T(128)} %constant.3.clone.1, s32[]{:T(128)} %constant.10.clone.1, s32[]{:T(128)} %constant.3.clone.1) | dynamic-update-slice | bytes 2359300 | tf_op jit(solution)/shard_map/dynamic_update_slice | solution.py:47
  107.0 3.3 %fusion.45 = f32[50,26,256]{2,1,0:T(8,128)} fusion(f32[50,26,256]{2,1,0:T(8,128)} %dynamic_update_slice.29, bf16[1,48,24,1024]{3,2,0,1:T(8,128)(2,1)S(1)} %copy-done, bf16[3,3,256,1024]{3,2,1,0:T(8,128)(2,1)} %param.4), kind=kOutput, calls=%fused_computation.40 | convolution fusion | flops 604274688 | bytes 5242880 | tf_op jit(solution)/shard_map/hwo,io->hwi/dot_general | solution.py:43
  110.3 2.4 %fusion.48 = f32[48,24,256]{2,1,0:T(8,128)S(1)} fusion(bf16[1,48,24,1024]{3,2,0,1:T(8,128)(2,1)S(1)} %copy-done, f32[50,26,256]{2,1,0:T(8,128)} %fusion.45, bf16[3,3,256,1024]{3,2,1,0:T(8,128)(2,1)} %param.4), kind=kOutput, calls=%fused_computation.41 | convolution fusion | flops 604274688 | bytes 5242880 | tf_op jit(solution)/shard_map/hwo,io->hwi/dot_general | solution.py:43
  112.8 7.0 %dynamic_update_slice.31 = f32[50,26,256]{2,1,0:T(8,128)} dynamic-update-slice(f32[50,26,256]{2,1,0:T(8,128)} %fusion.45, f32[48,24,256]{2,1,0:T(8,128)S(1)} %fusion.48, s32[]{:T(128)} %constant.4.clone.1, s32[]{:T(128)} %constant.4.clone.1, s32[]{:T(128)} %constant.3.clone.1) | dynamic-update-slice | bytes 2359300 | tf_op jit(solution)/shard_map/dynamic_update_slice | solution.py:47
  119.8 2.4 %fusion.51 = f32[48,24,256]{2,1,0:T(8,128)S(1)} fusion(bf16[1,48,24,1024]{3,2,0,1:T(8,128)(2,1)S(1)} %copy-done, f32[50,26,256]{2,1,0:T(8,128)} %dynamic_update_slice.31, bf16[3,3,256,1024]{3,2,1,0:T(8,128)(2,1)} %param.4), kind=kOutput, calls=%fused_computation.42 | convolution fusion | flops 604274688 | bytes 5242880 | tf_op jit(solution)/shard_map/hwo,io->hwi/dot_general | solution.py:43
  122.2 7.0 %dynamic_update_slice.32 = f32[50,26,256]{2,1,0:T(8,128)} dynamic-update-slice(f32[50,26,256]{2,1,0:T(8,128)} %dynamic_update_slice.31, f32[48,24,256]{2,1,0:T(8,128)S(1)} %fusion.51, s32[]{:T(128)} %constant.4.clone.1, s32[]{:T(128)} %constant.10.clone.1, s32[]{:T(128)} %constant.3.clone.1) | dynamic-update-slice | bytes 2359300 | tf_op jit(solution)/shard_map/dynamic_update_slice | solution.py:47
  129.3 3.4 %fusion.57 = f32[50,26,256]{2,1,0:T(8,128)} fusion(f32[50,26,256]{2,1,0:T(8,128)} %dynamic_update_slice.32, bf16[1,48,24,1024]{3,2,0,1:T(8,128)(2,1)S(1)} %copy-done, bf16[3,3,256,1024]{3,2,1,0:T(8,128)(2,1)} %param.4), kind=kOutput, calls=%fused_computation.44 | convolution fusion | flops 604274688 | bytes 5242880 | tf_op jit(solution)/shard_map/hwo,io->hwi/dot_general | solution.py:43
  132.7 2.4 %fusion.60 = f32[48,24,256]{2,1,0:T(8,128)S(1)} fusion(bf16[1,48,24,1024]{3,2,0,1:T(8,128)(2,1)S(1)} %copy-done, f32[50,26,256]{2,1,0:T(8,128)} %fusion.57, bf16[3,3,256,1024]{3,2,1,0:T(8,128)(2,1)} %param.4), kind=kOutput, calls=%fused_computation.45 | convolution fusion | flops 604274688 | bytes 5242880 | tf_op jit(solution)/shard_map/hwo,io->hwi/dot_general | solution.py:43
  135.1 7.0 %dynamic_update_slice.34 = f32[50,26,256]{2,1,0:T(8,128)} dynamic-update-slice(f32[50,26,256]{2,1,0:T(8,128)} %fusion.57, f32[48,24,256]{2,1,0:T(8,128)S(1)} %fusion.60, s32[]{:T(128)} %constant.10.clone.1, s32[]{:T(128)} %constant.4.clone.1, s32[]{:T(128)} %constant.3.clone.1) | dynamic-update-slice | bytes 2359300 | tf_op jit(solution)/shard_map/dynamic_update_slice | solution.py:47
  142.1 2.4 %fusion.63 = f32[48,24,256]{2,1,0:T(8,128)S(1)} fusion(bf16[1,48,24,1024]{3,2,0,1:T(8,128)(2,1)S(1)} %copy-done, f32[50,26,256]{2,1,0:T(8,128)} %dynamic_update_slice.34, bf16[3,3,256,1024]{3,2,1,0:T(8,128)(2,1)} %param.4), kind=kOutput, calls=%fused_computation.46 | convolution fusion | flops 604274688 | bytes 5242880 | tf_op jit(solution)/shard_map/hwo,io->hwi/dot_general | solution.py:43
  144.5 7.0 %dynamic_update_slice.35 = f32[50,26,256]{2,1,0:T(8,128)} dynamic-update-slice(f32[50,26,256]{2,1,0:T(8,128)} %dynamic_update_slice.34, f32[48,24,256]{2,1,0:T(8,128)S(1)} %fusion.63, s32[]{:T(128)} %constant.10.clone.1, s32[]{:T(128)} %constant.10.clone.1, s32[]{:T(128)} %constant.3.clone.1) | dynamic-update-slice | bytes 2359300 | tf_op jit(solution)/shard_map/dynamic_update_slice | solution.py:47
  151.5 2.4 %fusion.120 = bf16[1,48,24,256]{3,2,1,0:T(8,128)(2,1)} fusion(f32[50,26,256]{2,1,0:T(8,128)} %dynamic_update_slice.35), kind=kLoop, calls=%fused_computation.74 | loop fusion | bytes 1179648 | tf_op jit(solution)/shard_map/broadcast_in_dim | solution.py:58
  153.9 0.0 reduce-scatter.3.cloned.1.call-done
  153.9 2.2 convert_bitcast_fusion
  156.1 73.2 %reduce-scatter.5.cloned.1.call-done = f32[128,3,3,256]{3,0,2,1:T(8,128)} async-done(((f32[1024,3,3,256]{3,0,2,1:T(8,128)}), f32[128,3,3,256]{3,0,2,1:T(8,128)}) %reduce-scatter.5.cloned.1.call-update) | async-done | bytes 1179664 | tf_op jit(solution)/shard_map/reduce_scatter | solution.py:61
  229.3 2.4 %broadcast_multiply_fusion = f32[128,3,3,256]{3,0,2,1:T(8,128)} fusion(f32[128,3,3,256]{3,0,2,1:T(8,128)} %reduce-scatter.5.cloned.1.call-done), kind=kLoop, calls=%fused_computation.75 | loop fusion | flops 294912 | bytes 2359296 | tf_op jit(solution)/shard_map/mul | solution.py:62
Async XLA Ops:
  7.2 55.1 %all-gather.2.cloned.1.call-start = ((), (), s32[]{:S(2)}) async-start(), calls=%async_computation.3 | async-start | bytes 2949120 | tf_op jit(solution)/shard_map/all_gather | solution.py:38
  7.9 146.0 %reduce-scatter.3.cloned.1.call-start = ((), (), s32[]{:S(2)}) async-start(), calls=%async_computation.2 | async-start | bytes 5898240 | tf_op jit(solution)/shard_map/reduce_scatter | solution.py:29
  7.9 2.2 copy-start.1
  8.0 2.9 %copy-start.3 = (bf16[3,3,256,1024]{3,2,1,0:T(8,128)(2,1)S(1)}, bf16[3,3,256,1024]{3,2,1,0:T(8,128)(2,1)}, u32[]{:S(2)}) copy-start(bf16[3,3,256,1024]{3,2,1,0:T(8,128)(2,1)} %param.4) | copy-start | bytes 14155780
  42.5 186.9 %reduce-scatter.5.cloned.1.call-start = ((), (), s32[]{:S(2)}) async-start(), calls=%async_computation.4 | async-start | bytes 10616832 | tf_op jit(solution)/shard_map/reduce_scatter | solution.py:61
  62.3 2.7 %copy-start = (bf16[1,48,24,1024]{3,2,0,1:T(8,128)(2,1)S(1)}, bf16[1,48,24,1024]{3,2,0,1:T(8,128)(2,1)}, u32[]{:S(2)}) copy-start(bf16[1,48,24,1024]{3,2,0,1:T(8,128)(2,1)} %all-gather.2.cloned.1.call-done) | copy-start | bytes 7077892
  72.0 3.7 %copy-start.2 = (f32[1024,9,256]{0,2,1:T(8,128)}, f32[1024,9,256]{0,2,1:T(8,128)S(1)}, u32[]{:S(2)}) copy-start(f32[1024,9,256]{0,2,1:T(8,128)S(1)} %fusion.117) | copy-start | bytes 28311556
Sparse Core Ops, SparseCore 0:
  9.5 52.6 all-gather.1
  64.6 84.0 reduce-scatter.2
  152.2 77.1 reduce-scatter.4
where the time goes:
time: 240 us; the launch traced here: 238 us
  waiting for transfers between devices  93.5 us (39%)
  matrix products  66.1 us (28%)
  local copies, waits for them, and re-layouts  59.9 us (25%)
  between operations  13.9 us (6%)
  other arithmetic  4.56 us (2%)
    reduce_scatter x1, waiting for transfers between devices, on_device(): mine = lax.psum_scatter(grads, 'dp', scatter_dimension=0, tiled=True)  73.2 us
    dynamic_update_slice x7, local copies, waits for them, and re-layouts, on_device(): lax.dynamic_update_slice(back_pad, region + contrib, (start + a, b, 0))  43.5 us
    dot_general x9, matrix products, conv_rows(): jnp.einsum('hwi,io->hwo', xpad[a:a + count, b:b + width], weights[a, b],...  33.8 us
    dot_general x9, matrix products, on_device(): jnp.einsum('hwo,io->hwi', grad_rows, kernel[a, b], preferred_element_type...  22.6 us
    all_gather x1, waiting for transfers between devices, on_device(): grad_rows = lax.all_gather(cotangent, 'filter', axis=1, tiled=True)[0]  19.6 us
    dot_general x9, matrix products, on_device(): jnp.einsum('hwi,hwo->oi', xpad[a:a + count, b:b + width], grad_rows, pref...  9.7 us
    reshape x1, local copies, waits for them, and re-layouts, on_device(): grads = jnp.stack(taps, 1).reshape(channels, 3, 3, local_in)  9.63 us
  transfers between devices with their start and end apart: 3, of which 2 were waited for; matrix products, arithmetic and copies ran while one was open for 52% of the time, Pallas kernels for 0%

commit v1 on v0

--- a/solution.py
+++ b/solution.py
@@ -2,6 +2,18 @@
 import jax.numpy as jnp
 from jax import lax
 from jax.sharding import PartitionSpec as P
+
+
+def doubled_up(value, axis, dim):
+    ways, here, hop = (lax.axis_size(axis), lax.axis_index(axis), value.shape[dim])
+    line, have = (value, 1)
+    while have < ways:
+        line = jnp.concatenate(
+            [line, lax.ppermute(line, axis, [(d, (d - have) % ways) for d in range(ways)])],
+            axis=dim,
+        )
+        have = 2 * have
+    return jnp.roll(line, here * hop, axis=dim)
 
 
 def conv_rows(xpad, weights, count, width):
@@ -35,7 +47,7 @@
     outputs = summed.astype(jnp.bfloat16)[None]
     start = jnp.int32(0)
     back_pad = jnp.zeros((height + 2, width + 2, local_in), jnp.float32)
-    grad_rows = lax.all_gather(cotangent, "filter", axis=1, tiled=True)[0]
+    grad_rows = doubled_up(cotangent, "filter", 1)[0]
     count = grad_rows.shape[0]
     taps = []
     for a in range(3):

time: 240 us -> 289 us (1.20)
  waiting for transfers between devices: 93.5 us -> 129 us
  starting transfers between devices: 0.3 us -> 10.1 us
  local copies, waits for them, and re-layouts: 59.9 us -> 63.1 us
    ppermute x0 -> x2, waiting for transfers between devices: none -> 129 us  [doubled_up(): lax.ppermute(line, axis, [(d, (d - have) % ways) for d in range(ways)])]
    reduce_scatter x1, waiting for transfers between devices: 73.2 us -> 0.01 us  [on_device(): mine = lax.psum_scatter(grads, 'dp', scatter_dimension=0, tiled=True)]
    all_gather x1 -> x0, waiting for transfers between devices: 19.6 us -> none  [on_device(): grad_rows = lax.all_gather(cotangent, 'filter', axis=1, tiled=True)[0]]
    dynamic_update_slice x7, local copies, waits for them, and re-layouts: 43.5 us -> 56.2 us  [on_device(): lax.dynamic_update_slice(back_pad, region + contrib, (start + a, b, 0))]
    ppermute x0 -> x2, starting transfers between devices: none -> 10 us  [doubled_up(): lax.ppermute(line, axis, [(d, (d - have) % ways) for d in range(ways)])]
    reshape x1 -> x0, local copies, waits for them, and re-layouts: 9.63 us -> none  [on_device(): grads = jnp.stack(taps, 1).reshape(channels, 3, 3, local_in)]
  transfers between devices with their start and end apart: 3 -> 4, of which waited for: 2 -> 2; matrix products, arithmetic and copies ran while one was open for 52% -> 32% of each run, Pallas kernels for 0% -> 0%
where the time goes in v1:
time: 289 us; the launch traced here: 288 us
  waiting for transfers between devices  129 us (45%)
  matrix products  66.4 us (23%)
  local copies, waits for them, and re-layouts  63.1 us (22%)
  between operations  14.3 us (5%)
  starting transfers between devices  10.1 us (3%)
  other arithmetic  5.67 us (2%)
    ppermute x2, waiting for transfers between devices, doubled_up(): lax.ppermute(line, axis, [(d, (d - have) % ways) for d in range(ways)])  129 us
    dynamic_update_slice x7, local copies, waits for them, and re-layouts, on_device(): lax.dynamic_update_slice(back_pad, region + contrib, (start + a, b, 0))  56.2 us
    dot_general x9, matrix products, conv_rows(): jnp.einsum('hwi,io->hwo', xpad[a:a + count, b:b + width], weights[a, b],...  33.6 us
    dot_general x9, matrix products, on_device(): jnp.einsum('hwo,io->hwi', grad_rows, kernel[a, b], preferred_element_type...  24.4 us
    ppermute x2, starting transfers between devices, doubled_up(): lax.ppermute(line, axis, [(d, (d - have) % ways) for d in range(ways)])  10 us
    dot_general x9, matrix products, on_device(): jnp.einsum('hwi,hwo->oi', xpad[a:a + count, b:b + width], grad_rows, pref...  8.36 us
  transfers between devices with their start and end apart: 4, of which 2 were waited for; matrix products, arithmetic and copies ran while one was open for 32% of the time, Pallas kernels for 0%

profile of v1, /device:TPU:0, one launch (start us, length us, event | category | flops | bytes accessed | tf_op | source)
XLA Modules:
  0.0 288.3 jit_solution(10825635736482715284)
XLA Ops:
  7.2 0.0 copy-start
  7.2 0.0 reduce-scatter.3.cloned.1.call-start
  7.2 0.0 copy-start.3
  7.2 2.2 fusion.111
  9.4 0.0 copy-done
  9.4 0.6 copy-done.3
  10.0 0.8 fusion.118
  10.8 3.0 %fusion.121 = f32[48,24,1024]{2,1,0:T(8,128)} fusion(bf16[3,3,256,1024]{3,2,1,0:T(8,128)(2,1)S(1)} %copy-done.3, bf16[48,24,256]{2,1,0:T(8,128)(2,1)S(1)} %bitcast.221), kind=kOutput, calls=%fused_computation.87 | convolution fusion | flops 603979776 | bytes 5832704 | tf_op jit(solution)/shard_map/hwi,io->hwo/dot_general | solution.py:23
  13.9 2.9 %fusion.128 = f32[48,24,1024]{2,1,0:T(8,128)} fusion(bf16[3,3,256,1024]{3,2,1,0:T(8,128)(2,1)S(1)} %copy-done.3, bf16[1,48,24,256]{3,2,1,0:T(8,128)(2,1)S(1)} %copy-done), kind=kOutput, calls=%fused_computation.90 | convolution fusion | flops 603979776 | bytes 5832704 | tf_op jit(solution)/shard_map/hwi,io->hwo/dot_general | solution.py:23
  16.8 3.0 %fusion.131 = f32[48,24,1024]{2,1,0:T(8,128)} fusion(bf16[3,3,256,1024]{3,2,1,0:T(8,128)(2,1)S(1)} %copy-done.3, bf16[48,24,256]{2,1,0:T(8,128)(2,1)S(1)} %bitcast.222), kind=kOutput, calls=%fused_computation.93 | convolution fusion | flops 603979776 | bytes 5832704 | tf_op jit(solution)/shard_map/hwi,io->hwo/dot_general | solution.py:23
  19.7 3.0 %fusion.138 = f32[48,24,1024]{2,1,0:T(8,128)} fusion(bf16[3,3,256,1024]{3,2,1,0:T(8,128)(2,1)S(1)} %copy-done.3, bf16[48,24,256]{2,1,0:T(8,128)(2,1)S(1)} %bitcast.223), kind=kOutput, calls=%fused_computation.96 | convolution fusion | flops 603979776 | bytes 5832704 | tf_op jit(solution)/shard_map/hwi,io->hwo/dot_general | solution.py:23
  22.7 2.9 %fusion.148 = f32[48,24,1024]{2,1,0:T(8,128)} fusion(bf16[3,3,256,1024]{3,2,1,0:T(8,128)(2,1)S(1)} %copy-done.3, bf16[48,24,256]{2,1,0:T(8,128)(2,1)S(1)} %bitcast.224), kind=kOutput, calls=%fused_computation.102 | convolution fusion | flops 603979776 | bytes 5832704 | tf_op jit(solution)/shard_map/hwi,io->hwo/dot_general | solution.py:23
  25.7 3.0 %fusion.141 = f32[48,24,1024]{2,1,0:T(8,128)} fusion(bf16[3,3,256,1024]{3,2,1,0:T(8,128)(2,1)S(1)} %copy-done.3, bf16[48,24,256]{2,1,0:T(8,128)(2,1)S(1)} %bitcast.225), kind=kOutput, calls=%fused_computation.99 | convolution fusion | flops 603979776 | bytes 5832704 | tf_op jit(solution)/shard_map/hwi,io->hwo/dot_general | solution.py:23
  28.6 12.9 %add_add_fusion = f32[48,24,1024]{2,1,0:T(8,128)} fusion(f32[48,24,1024]{2,1,0:T(8,128)S(1)} %fusion.111, f32[48,24,1024]{2,1,0:T(8,128)S(1)} %fusion.118, f32[48,24,1024]{2,1,0:T(8,128)} %fusion.121, f32[48,24,1024]{2,1,0:T(8,128)} %fusion.128, f32[48,24,1024]{2,1,0:T(8,128)} %fusion.131, f32[48,24,1024]{2,1,0:T(8,128)} %fusion.138, ...), kind=kOutput, calls=%fused_computation | convolution fusion | flops 613416960 | bytes 43581440 | tf_op jit(solution)/shard_map/hwi,io->hwo/dot_general | solution.py:23
  41.5 0.0 copy-start.5
  41.5 0.0 reduce-scatter.3.cloned.1.call-update
  41.6 0.0 reduce-scatter.5.cloned.1.call-start
  41.6 1.0 copy-done.5
  42.6 5.1 %collective-permute-start = (bf16[1,12,24,1024]{3,2,1,0:T(8,128)(2,1)S(1)}, bf16[1,12,24,1024]{3,2,1,0:T(8,128)(2,1)S(1)}, u32[]{:S(2)}, u32[]{:S(2)}) collective-permute-start(bf16[1,12,24,1024]{3,2,1,0:T(8,128)(2,1)S(1)} %copy-done.5), channel_id=1, source_target_pairs={{0,3},{1,0},{2,1},{3,2},{4,7},{5,4},{6,5},{7,6},{8,11},{9,8},{10,9... | collective-permute-start | bytes 1769480 | tf_op jit(solution)/shard_map/ppermute | solution.py:12
  47.7 25.0 %collective-permute-done = bf16[1,12,24,1024]{3,2,1,0:T(8,128)(2,1)S(1)} collective-permute-done((bf16[1,12,24,1024]{3,2,1,0:T(8,128)(2,1)S(1)}, bf16[1,12,24,1024]{3,2,1,0:T(8,128)(2,1)S(1)}, u32[]{:S(2)}, u32[]{:S(2)}) %collective-permute-start) | collective-permute-done | bytes 589856 | tf_op jit(solution)/shard_map/ppermute | solution.py:12
  72.7 1.1 pad_maximum_fusion
  73.8 5.0 %collective-permute-start.1 = (bf16[1,24,24,1024]{3,2,1,0:T(8,128)(2,1)}, bf16[1,24,24,1024]{3,2,1,0:T(8,128)(2,1)S(1)}, u32[]{:S(2)}, u32[]{:S(2)}) collective-permute-start(bf16[1,24,24,1024]{3,2,1,0:T(8,128)(2,1)} %pad_maximum_fusion), channel_id=1, source_target_pairs={{0,2},{1,3},{2,0},{3,1},{4,6},{5,7},{6,4},{7,5},{8,10},{9,11},{10,... | collective-permute-start | bytes 3538952 | tf_op jit(solution)/shard_map/ppermute | solution.py:12
  78.9 103.7 %collective-permute-done.1 = bf16[1,24,24,1024]{3,2,1,0:T(8,128)(2,1)S(1)} collective-permute-done((bf16[1,24,24,1024]{3,2,1,0:T(8,128)(2,1)}, bf16[1,24,24,1024]{3,2,1,0:T(8,128)(2,1)S(1)}, u32[]{:S(2)}, u32[]{:S(2)}) %collective-permute-start.1) | collective-permute-done | bytes 1179680 | tf_op jit(solution)/shard_map/ppermute | solution.py:12
  182.5 0.1 constant_dynamic-update-slice_fusion.3
  182.7 0.1 constant_dynamic-update-slice_fusion
  182.8 0.0 copy-start.1
  182.8 0.9 fusion.51
  183.7 0.9 fusion.57
  184.7 0.9 fusion.63
  185.6 0.9 fusion.69
  186.5 0.9 fusion.75
  187.5 0.9 fusion.81
  188.4 0.9 fusion.87
  189.4 0.9 fusion.93
  190.3 0.0 copy-done.1
  190.3 0.9 fusion.99
  191.2 0.0 copy-start.4
  191.3 3.6 %copy-done.4 = f32[1024,9,256]{2,0,1:T(8,128)} copy-done((f32[1024,9,256]{2,0,1:T(8,128)}, f32[1024,9,256]{2,0,1:T(8,128)S(1)}, u32[]{:S(2)}) %copy-start.4) | copy-done | bytes 9437208
  194.9 0.0 reduce-scatter.5.cloned.1.call-update
  194.9 0.0 copy-start.2
  194.9 2.7 fusion.34
  197.6 0.2 dynamic_update_slice.27
  197.8 0.3 copy-done.2
  198.1 1.9 slice_add_fusion.4
  200.0 9.7 %dynamic_update_slice.28 = f32[50,26,256]{2,1,0:T(8,128)S(1)} dynamic-update-slice(f32[50,26,256]{2,1,0:T(8,128)S(1)} %dynamic_update_slice.27, f32[48,24,256]{2,1,0:T(8,128)S(1)} %slice_add_fusion.4, s32[]{:T(128)} %constant.27.clone.1, s32[]{:T(128)} %constant.33.clone.1, s32[]{:T(128)} %constant.27.clone.1) | dynamic-update-slice | bytes 2359300 | tf_op jit(solution)/shard_map/dynamic_update_slice | solution.py:59
  209.7 3.2 %fusion.36 = f32[48,24,256]{2,1,0:T(8,128)S(1)} fusion(f32[50,26,256]{2,1,0:T(8,128)S(1)} %dynamic_update_slice.28, bf16[3,3,256,1024]{3,2,1,0:T(8,128)(2,1)} %param.4, bf16[1,96,24,1024]{3,2,1,0:T(8,128)(2,1)} %copy-done.1, s32[]{:T(128)S(6)} %select_n.14), kind=kOutput, calls=%fused_computation.37 | convolution fusion | flops 604274688 | bytes 5242884 | tf_op jit(solution)/shard_map/hwo,io->hwi/dot_general | solution.py:55
  212.9 9.4 %dynamic_update_slice.29 = f32[50,26,256]{2,1,0:T(8,128)S(1)} dynamic-update-slice(f32[50,26,256]{2,1,0:T(8,128)S(1)} %dynamic_update_slice.28, f32[48,24,256]{2,1,0:T(8,128)S(1)} %fusion.36, s32[]{:T(128)} %constant.27.clone.1, s32[]{:T(128)} %constant.34.clone.1, s32[]{:T(128)} %constant.27.clone.1) | dynamic-update-slice | bytes 2359300 | tf_op jit(solution)/shard_map/dynamic_update_slice | solution.py:59
  222.4 3.4 %fusion.102 = f32[50,26,256]{2,1,0:T(8,128)S(1)} fusion(f32[50,26,256]{2,1,0:T(8,128)S(1)} %dynamic_update_slice.29, bf16[3,3,256,1024]{3,2,1,0:T(8,128)(2,1)} %param.4, bf16[1,96,24,1024]{3,2,1,0:T(8,128)(2,1)} %copy-done.1, s32[]{:T(128)S(6)} %select_n.14), kind=kOutput, calls=%fused_computation.64 | convolution fusion | flops 604274688 | bytes 5242884 | tf_op jit(solution)/shard_map/hwo,io->hwi/dot_general | solution.py:55
  225.8 2.6 fusion.39
  228.4 9.3 %dynamic_update_slice.31 = f32[50,26,256]{2,1,0:T(8,128)S(1)} dynamic-update-slice(f32[50,26,256]{2,1,0:T(8,128)S(1)} %fusion.102, f32[48,24,256]{2,1,0:T(8,128)S(1)} %fusion.39, s32[]{:T(128)} %constant.33.clone.1, s32[]{:T(128)} %constant.33.clone.1, s32[]{:T(128)} %constant.27.clone.1) | dynamic-update-slice | bytes 2359300 | tf_op jit(solution)/shard_map/dynamic_update_slice | solution.py:59
  237.7 2.6 slice_add_fusion.2
  240.3 9.3 %dynamic_update_slice.32 = f32[50,26,256]{2,1,0:T(8,128)S(1)} dynamic-update-slice(f32[50,26,256]{2,1,0:T(8,128)S(1)} %dynamic_update_slice.31, f32[48,24,256]{2,1,0:T(8,128)S(1)} %slice_add_fusion.2, s32[]{:T(128)} %constant.33.clone.1, s32[]{:T(128)} %constant.34.clone.1, s32[]{:T(128)} %constant.27.clone.1) | dynamic-update-slice | bytes 2359300 | tf_op jit(solution)/shard_map/dynamic_update_slice | solution.py:59
  249.6 2.8 fusion.45
  252.4 2.6 slice_add_fusion.1
  255.0 9.2 %dynamic_update_slice.34 = f32[50,26,256]{2,1,0:T(8,128)S(1)} dynamic-update-slice(f32[50,26,256]{2,1,0:T(8,128)S(1)} %fusion.45, f32[48,24,256]{2,1,0:T(8,128)S(1)} %slice_add_fusion.1, s32[]{:T(128)} %constant.34.clone.1, s32[]{:T(128)} %constant.33.clone.1, s32[]{:T(128)} %constant.27.clone.1) | dynamic-update-slice | bytes 2359300 | tf_op jit(solution)/shard_map/dynamic_update_slice | solution.py:59
  264.2 2.6 slice_add_fusion
  266.8 9.2 %dynamic_update_slice.35 = f32[50,26,256]{2,1,0:T(8,128)S(1)} dynamic-update-slice(f32[50,26,256]{2,1,0:T(8,128)S(1)} %dynamic_update_slice.34, f32[48,24,256]{2,1,0:T(8,128)S(1)} %slice_add_fusion, s32[]{:T(128)} %constant.34.clone.1, s32[]{:T(128)} %constant.34.clone.1, s32[]{:T(128)} %constant.27.clone.1) | dynamic-update-slice | bytes 2359300 | tf_op jit(solution)/shard_map/dynamic_update_slice | solution.py:59
  275.9 1.0 fusion.103
  276.9 0.0 reduce-scatter.3.cloned.1.call-done
  276.9 2.2 convert_bitcast_fusion
  279.1 0.0 reduce-scatter.5.cloned.1.call-done
  279.1 2.4 broadcast_multiply_fusion
  (4 shorter events, 0.2 us)
Async XLA Ops:
  7.2 2.2 copy-start
  7.2 269.8 %reduce-scatter.3.cloned.1.call-start = ((), (), s32[]{:S(2)}) async-start(), calls=%async_computation.2 | async-start | bytes 5898240 | tf_op jit(solution)/shard_map/reduce_scatter | solution.py:41
  7.2 2.8 copy-start.3
  41.5 1.1 copy-start.5
  41.6 237.6 %reduce-scatter.5.cloned.1.call-start = ((), (), s32[]{:S(2)}) async-start(), calls=%async_computation.3 | async-start | bytes 10616832 | tf_op jit(solution)/shard_map/reduce_scatter | solution.py:73
  42.6 30.1 %collective-permute-start = (bf16[1,12,24,1024]{3,2,1,0:T(8,128)(2,1)S(1)}, bf16[1,12,24,1024]{3,2,1,0:T(8,128)(2,1)S(1)}, u32[]{:S(2)}, u32[]{:S(2)}) collective-permute-start(bf16[1,12,24,1024]{3,2,1,0:T(8,128)(2,1)S(1)} %copy-done.5), channel_id=1, source_target_pairs={{0,3},{1,0},{2,1},{3,2},{4,7},{5,4},{6,5},{7,6},{8,11},{9,8},{10,9... | collective-permute-start | bytes 1769480 | tf_op jit(solution)/shard_map/ppermute | solution.py:12
  73.8 108.7 %collective-permute-start.1 = (bf16[1,24,24,1024]{3,2,1,0:T(8,128)(2,1)}, bf16[1,24,24,1024]{3,2,1,0:T(8,128)(2,1)S(1)}, u32[]{:S(2)}, u32[]{:S(2)}) collective-permute-start(bf16[1,24,24,1024]{3,2,1,0:T(8,128)(2,1)} %pad_maximum_fusion), channel_id=1, source_target_pairs={{0,2},{1,3},{2,0},{3,1},{4,6},{5,7},{6,4},{7,5},{8,10},{9,11},{10,... | collective-permute-start | bytes 3538952 | tf_op jit(solution)/shard_map/ppermute | solution.py:12
  182.8 7.5 %copy-start.1 = (bf16[1,96,24,1024]{3,2,1,0:T(8,128)(2,1)}, bf16[1,96,24,1024]{3,2,1,0:T(8,128)(2,1)S(1)}, u32[]{:S(2)}) copy-start(bf16[1,96,24,1024]{3,2,1,0:T(8,128)(2,1)S(1)} %constant_dynamic-update-slice_fusion) | copy-start | bytes 14155780
  191.2 3.6 %copy-start.4 = (f32[1024,9,256]{2,0,1:T(8,128)}, f32[1024,9,256]{2,0,1:T(8,128)S(1)}, u32[]{:S(2)}) copy-start(f32[1024,9,256]{2,0,1:T(8,128)S(1)} %fusion.99) | copy-start | bytes 28311556
  194.9 3.2 %copy-start.2 = (bf16[1,96,24,1024]{3,2,1,0:T(8,128)(2,1)S(1)}, bf16[1,96,24,1024]{3,2,1,0:T(8,128)(2,1)}, u32[]{:S(2)}) copy-start(bf16[1,96,24,1024]{3,2,1,0:T(8,128)(2,1)} %copy-done.1) | copy-start | bytes 14155780
Sparse Core Ops, SparseCore 0:
  41.7 135.4 reduce-scatter.2
  195.0 78.4 reduce-scatter.4
